TPU v7x, 32 devices: a whole 2x2x4 slice. The times are simulated.
32 devices in a mesh: groups: 2 (over y), expert: 16 (over z, x, core).
Axes of the slice: x: 2, y: 2, z: 4, core: 2. Of those that a mesh axis runs over, the one named last changes fastest.
Arguments:
- activations: bfloat16 [2, 512, 2048], P(None, ('groups', 'expert')), parts along dimension 1, may hold values from -6 to 6
- pick_weight: float32 [2, 512, 1], P(None, ('groups', 'expert')), parts along dimension 1, may hold values from 0.2 to 1
- expert_ids: int32 [2, 512, 1], P(None, ('groups', 'expert')), parts along dimension 1, may hold values from 0 to 7, as said below
- replica: int32 [2, 512, 1], P(None, ('groups', 'expert')), parts along dimension 1, may hold values from 0 to 4, as said below
- old_home: int32 [8], replicated, may hold values from 0 to 7, each once
- new_expert: int32 [32], P('groups'), parts along dimension 0, may hold values from 0 to 7, as said below
- gate_panel: bfloat16 [16, 2048, 384], P('expert'), may hold values from -0.125 to 0.125
- up_panel: bfloat16 [16, 2048, 384], P('expert'), may hold values from -0.125 to 0.125
- down_panel: bfloat16 [16, 2048, 384], P('expert'), may hold values from -0.21875 to 0.21875
Outputs:
- layer_output: bfloat16 [2, 512, 2048], P(None, ('groups', 'expert')), parts along dimension 1
- slot_load: int32 [32], P(('groups', 'expert')), parts along dimension 0
There are 2 independent parts, one for each index of `groups`. A program takes and returns all parts, laid end to end along the dimension named above; an argument that names none is the same for every part. Nothing has to cross between parts.
Inputs may be any that keep to these rules, and one draw needn't show every extreme that they name: `new_expert`: every expert is held by 1 or 5 slots. `expert_ids`: the 1 expert that a token names are different. replica[s, t, k] is below the number of slots that new_expert gives to expert_ids[s, t, k]. The picks of the 16 tokens of one device in one batch that land on one slot number at most 2, and in each batch some slot receives exactly 2 from every device.
All inputs are finite; a program needn't handle non-finite values.
Results may differ from a plain program's by a relative error of at most 0.0057.
Values may be sent and summed in bfloat16 or wider, within the bound.
No kernel may reach another device: no remote copies, remote signals or barrier semaphores. Data moves between devices by JAX's collectives and lax.ppermute only.
A program may use at most 128 MiB of HBM per device.

v0:
```python
import jax
import jax.numpy as jnp
from jax import lax
from jax.sharding import PartitionSpec as P

CAP = 2


def slot_ranks(new_expert):
    count = new_expert.shape[0]
    positions = jnp.arange(count, dtype=jnp.int32)
    same = new_expert[:, None] == new_expert[None, :]
    earlier = positions[None, :] < positions[:, None]
    return jnp.sum((same & earlier).astype(jnp.int32), axis=1)


def expert_rows(picked, gate_full, up_full, down_full):
    gate = jnp.dot(picked, gate_full, preferred_element_type=jnp.float32)
    up_sum = jnp.dot(picked, up_full, preferred_element_type=jnp.float32)
    hidden = (jax.nn.silu(gate) * up_sum).astype(jnp.bfloat16)
    result = lax.dot_general(
        hidden, down_full, (((1,), (1,)), ((), ())), preferred_element_type=jnp.float32
    )
    return result.astype(jnp.bfloat16)


def route(tokens, ids, replica, new_expert, ranks):
    slots = new_expert.shape[0]
    per_token = ids.shape[1]
    picks = ids.shape[0] * per_token
    flat_ids = ids.reshape(picks)
    flat_rep = replica.reshape(picks)
    match = (new_expert[None, :] == flat_ids[:, None]) & (ranks[None, :] == flat_rep[:, None])
    match_int = match.astype(jnp.int32)
    slot_index = jnp.sum(match_int * jnp.arange(slots, dtype=jnp.int32)[None, :], axis=1)
    before = jnp.cumsum(match_int, axis=0) - match_int
    position = jnp.sum(before * match_int, axis=1)
    target = slot_index * CAP + position
    places = jnp.arange(slots * CAP, dtype=jnp.int32)
    chosen = (target[None, :] == places[:, None]).astype(jnp.int32)
    live = jnp.sum(chosen, axis=1)
    owner = jnp.arange(picks, dtype=jnp.int32) // per_token
    source = jnp.sum(chosen * owner[None, :], axis=1)
    sent = jnp.where(live[:, None] > 0, tokens[source], jnp.zeros((), tokens.dtype))
    return (sent.reshape(slots, CAP, tokens.shape[1]), live.reshape(slots, CAP), target)


def combine(back, target, weights):
    flat = back.reshape(-1, back.shape[-1])
    picked = flat[target].reshape(weights.shape[0], weights.shape[1], -1)
    total = jnp.sum(weights[:, :, None] * picked.astype(jnp.float32), axis=1)
    return total.astype(jnp.bfloat16)


def per_device(
    activations,
    pick_weight,
    expert_ids,
    replica,
    old_home,
    new_expert,
    gate_panel,
    up_panel,
    down_panel,
):
    slots = lax.axis_size("expert")
    width = gate_panel.shape[1]
    half = gate_panel.shape[2]
    block = width // slots
    ranks = slot_ranks(new_expert)
    batches = activations.shape[0]
    routed = [
        route(activations[batch], expert_ids[batch], replica[batch], new_expert, ranks)
        for batch in range(batches)
    ]
    sent_all = jnp.concatenate([item[0] for item in routed], axis=1)
    live_all = jnp.concatenate([item[1] for item in routed], axis=1)
    early_cells, early_marks = (
        lax.all_to_all(sent_all, "expert", split_axis=0, concat_axis=0, tiled=True),
        lax.all_to_all(live_all, "expert", split_axis=0, concat_axis=0, tiled=True),
    )
    gate_rows, up_rows, down_rows = (
        lax.all_to_all(
            gate_panel.reshape(slots, block, half),
            "expert",
            split_axis=0,
            concat_axis=0,
            tiled=True,
        ),
        lax.all_to_all(
            up_panel.reshape(slots, block, half), "expert", split_axis=0, concat_axis=0, tiled=True
        ),
        lax.all_to_all(
            down_panel.reshape(slots, block, half),
            "expert",
            split_axis=0,
            concat_axis=0,
            tiled=True,
        ),
    )
    labels = jnp.arange(old_home.shape[0], dtype=jnp.int32)
    home = jnp.sum(
        (new_expert[:, None] == labels[None, :]).astype(jnp.int32) * old_home[None, :], axis=1
    )
    first = 2 * home
    second = first + 1

    def deliver(pieces):
        return jnp.stack(
            (jnp.take(pieces, first, axis=0), jnp.take(pieces, second, axis=0)), axis=2
        )

    gate_full, up_full, down_full = (
        lax.all_to_all(deliver(gate_rows), "expert", split_axis=0, concat_axis=0, tiled=True),
        lax.all_to_all(deliver(up_rows), "expert", split_axis=0, concat_axis=0, tiled=True),
        lax.all_to_all(deliver(down_rows), "expert", split_axis=0, concat_axis=0, tiled=True),
    )
    gate_full = gate_full.reshape(width, 2 * half)
    up_full = up_full.reshape(width, 2 * half)
    down_full = down_full.reshape(width, 2 * half)
    outputs = []
    marks = early_marks
    done = expert_rows(early_cells.reshape(-1, width), gate_full, up_full, down_full)
    done, marks = (done.reshape(early_cells.shape), marks)
    back = lax.all_to_all(done, "expert", split_axis=0, concat_axis=0, tiled=True)
    load = jnp.sum(marks)
    for batch in range(batches):
        outputs.append(
            combine(back[:, batch * CAP : (batch + 1) * CAP], routed[batch][2], pick_weight[batch])
        )
    return (jnp.stack(outputs, axis=0), load.astype(jnp.int32).reshape(1))


def solution(mesh):
    return jax.shard_map(
        per_device,
        mesh=mesh,
        in_specs=(
            P(None, ("groups", "expert"), None),
            P(None, ("groups", "expert"), None),
            P(None, ("groups", "expert"), None),
            P(None, ("groups", "expert"), None),
            P(),
            P("groups"),
            P("expert", None, None),
            P("expert", None, None),
            P("expert", None, None),
        ),
        out_specs=(P(None, ("groups", "expert"), None), P(("groups", "expert"))),
        check_vma=False,
    )
```

profile of v0, /device:TPU:0, one launch (start us, length us, event | category | flops | bytes accessed | tf_op | source)
XLA Modules:
  0.0 406.1 jit_solution(18082761906989629838)
XLA Ops:
  0.6 43.3 %all_to_all.49 = bf16[16,128,384]{2,1,0:T(8,128)(2,1)S(1)} all-to-all(bf16[16,128,384]{2,1,0:T(8,128)(2,1)} %bitcast.90), channel_id=1, replica_groups=mesh['groups'=2,'expert'=16] {'expert'}, dimensions={0} | all-to-all | bytes 3145728 | tf_op jit(solution)/shard_map/all_to_all | solution.py:90
  44.0 5.2 %all-to-all-start.5 = ((bf16[16,128,384]{2,1,0:T(8,128)(2,1)}), bf16[16,128,384]{2,1,0:T(8,128)(2,1)S(1)}, u32[]{:S(2)}, u32[]{:S(2)}) async-start(bf16[16,128,384]{2,1,0:T(8,128)(2,1)} %bitcast.91), calls=%async_computation.5 | async-start | bytes 3145728 | tf_op jit(solution)/shard_map/all_to_all | solution.py:93
  51.6 29.4 %all-to-all-done.5 = bf16[16,128,384]{2,1,0:T(8,128)(2,1)S(1)} async-done(((bf16[16,128,384]{2,1,0:T(8,128)(2,1)}), bf16[16,128,384]{2,1,0:T(8,128)(2,1)S(1)}, u32[]{:S(2)}, u32[]{:S(2)}) %all-to-all-start.5) | async-done | bytes 1572896 | tf_op jit(solution)/shard_map/all_to_all | solution.py:93
  81.0 9.3 %all-to-all-start.1 = ((bf16[16,128,384]{2,1,0:T(8,128)(2,1)}), bf16[16,128,384]{2,1,0:T(8,128)(2,1)}, u32[]{:S(2)}, u32[]{:S(2)}) async-start(bf16[16,128,384]{2,1,0:T(8,128)(2,1)} %bitcast.92), calls=%async_computation.1 | async-start | bytes 3145728 | tf_op jit(solution)/shard_map/all_to_all | solution.py:83
  97.0 1.9 gather_fusion.9
  98.9 1.9 gather_fusion.8
  100.8 1.9 gather_fusion.7
  102.8 1.9 gather_fusion.6
  104.7 17.5 %all-to-all-done.1 = bf16[16,128,384]{2,1,0:T(8,128)(2,1)} async-done(((bf16[16,128,384]{2,1,0:T(8,128)(2,1)}), bf16[16,128,384]{2,1,0:T(8,128)(2,1)}, u32[]{:S(2)}, u32[]{:S(2)}) %all-to-all-start.1) | async-done | bytes 1572896 | tf_op jit(solution)/shard_map/all_to_all | solution.py:83
  122.2 9.1 %all-to-all-start = ((bf16[16,4,2048]{2,1,0:T(4,128)(2,1)}), bf16[16,4,2048]{2,1,0:T(4,128)(2,1)S(1)}, u32[]{:S(2)}, u32[]{:S(2)}) async-start(bf16[16,4,2048]{2,1,0:T(4,128)(2,1)} %pad_maximum_fusion.3), calls=%async_computation | async-start | bytes 524288 | tf_op jit(solution)/shard_map/all_to_all | solution.py:79
  131.3 3.5 gather_fusion.4
  134.8 3.6 gather_fusion.5
  138.4 4.9 %select_bitcast_fusion.4 = (bf16[16,128,1,384]{3,1,0,2:T(8,128)(2,1)S(1)}, bf16[16,128,1,384]{3,1,0,2:T(8,128)(2,1)}, bf16[16,128,1,384]{3,1,0,2:T(8,128)(2,1)},...) fusion(bf16[16,128,384]{2,1,0:T(8,128)(2,1)} %gather_fusion.5, ...), kind=kLoop, calls=%fused_computation.27 | loop fusion | flops 4718592 | bytes 18874400 | tf_op jit(solution)/shard_map/stack | solution.py:109
  143.6 2.2 copy.26
  145.8 6.0 %all-to-all-start.2 = ((bf16[16,128,2,384]{3,1,2,0:T(8,128)(2,1)}), bf16[16,128,2,384]{3,1,2,0:T(8,128)(2,1)S(1)}, u32[]{:S(2)}, u32[]{:S(2)}) async-start(bf16[16,128,2,384]{3,1,2,0:T(8,128)(2,1)} %copy.26), calls=%async_computation.2 | async-start | bytes 6291456 | tf_op jit(solution)/shard_map/all_to_all | solution.py:114
  151.8 2.2 pad_maximum_fusion.1
  154.1 2.2 copy.28
  156.2 54.8 %all-to-all-done.2 = bf16[16,128,2,384]{3,1,2,0:T(8,128)(2,1)S(1)} async-done(((bf16[16,128,2,384]{3,1,2,0:T(8,128)(2,1)}), bf16[16,128,2,384]{3,1,2,0:T(8,128)(2,1)S(1)}, u32[]{:S(2)}, u32[]{:S(2)}) %all-to-all-start.2) | async-done | bytes 3145760 | tf_op jit(solution)/shard_map/all_to_all | solution.py:114
  211.1 15.5 %all-to-all-start.4 = ((bf16[16,128,2,384]{3,1,2,0:T(8,128)(2,1)}), bf16[16,128,2,384]{3,1,2,0:T(8,128)(2,1)}, u32[]{:S(2)}, u32[]{:S(2)}) async-start(bf16[16,128,2,384]{3,1,2,0:T(8,128)(2,1)} %copy.28), calls=%async_computation.4 | async-start | bytes 6291456 | tf_op jit(solution)/shard_map/all_to_all | solution.py:115
  226.6 2.2 pad_maximum_fusion.2
  228.8 2.2 copy.30
  231.0 54.9 %all-to-all-done.4 = bf16[16,128,2,384]{3,1,2,0:T(8,128)(2,1)} async-done(((bf16[16,128,2,384]{3,1,2,0:T(8,128)(2,1)}), bf16[16,128,2,384]{3,1,2,0:T(8,128)(2,1)}, u32[]{:S(2)}, u32[]{:S(2)}) %all-to-all-start.4) | async-done | bytes 3145760 | tf_op jit(solution)/shard_map/all_to_all | solution.py:115
  285.8 15.5 %all-to-all-start.6 = ((bf16[16,128,2,384]{3,1,2,0:T(8,128)(2,1)}), bf16[16,128,2,384]{3,1,2,0:T(8,128)(2,1)}, u32[]{:S(2)}, u32[]{:S(2)}) async-start(bf16[16,128,2,384]{3,1,2,0:T(8,128)(2,1)} %copy.30), calls=%async_computation.6 | async-start | bytes 6291456 | tf_op jit(solution)/shard_map/all_to_all | solution.py:116
  303.0 3.5 copy.27
  306.5 4.1 %copy.29 = bf16[16,128,2,384]{1,0,3,2:T(8,128)(2,1)S(1)} copy(bf16[16,128,2,384]{3,1,2,0:T(8,128)(2,1)} %all-to-all-done.4) | data formatting | bytes 6291456 | tf_op jit(solution)/shard_map/all_to_all | solution.py:115
  310.7 3.7 fusion.6
  314.3 46.3 %all-to-all-done.6 = bf16[16,128,2,384]{3,1,2,0:T(8,128)(2,1)} async-done(((bf16[16,128,2,384]{3,1,2,0:T(8,128)(2,1)}), bf16[16,128,2,384]{3,1,2,0:T(8,128)(2,1)}, u32[]{:S(2)}, u32[]{:S(2)}) %all-to-all-start.6) | async-done | bytes 3145760 | tf_op jit(solution)/shard_map/all_to_all | solution.py:116
  360.6 15.4 %all-to-all-start.8 = ((s32[16,1,4]{2,1,0:T(1,128)}), s32[16,1,4]{2,1,0:T(1,128)S(1)}, u32[]{:S(2)}, u32[]{:S(2)}) async-start(s32[16,1,4]{2,1,0:T(1,128)} %copy.34), calls=%async_computation.8 | async-start | bytes 16384 | tf_op jit(solution)/shard_map/all_to_all | solution.py:80
  376.1 5.1 %copy.31 = bf16[16,128,2,384]{1,0,3,2:T(8,128)(2,1)} copy(bf16[16,128,2,384]{3,1,2,0:T(8,128)(2,1)} %all-to-all-done.6) | data formatting | bytes 6291456 | tf_op jit(solution)/shard_map/all_to_all | solution.py:116
  381.2 4.8 %fusion.9 = bf16[64,2048]{1,0:T(8,128)(2,1)} fusion(bf16[96,8,16,128]{3,2,1,0:T(8,128)(2,1)} %bitcast.88, bf16[64,2048]{1,0:T(8,128)(2,1)S(1)} %copy-done.2, bf16[96,8,16,128]{3,2,1,0:T(8,128)(2,1)S(1)} %bitcast.87, f32[64,768]{1,0:T(8,128)} %fusion.6), kind=kOutput, calls=%fused_computation.22 | convolution fusion | flops 403079168 | bytes 7012352 | tf_op jit(solution)/shard_map/dot_general | solution.py:21
  387.8 6.0 %all-to-all-start.7 = ((bf16[16,4,2048]{2,1,0:T(4,128)(2,1)}), bf16[16,4,2048]{2,1,0:T(4,128)(2,1)S(1)}, u32[]{:S(2)}, u32[]{:S(2)}) async-start(bf16[16,4,2048]{2,1,0:T(4,128)(2,1)} %reshape.278), calls=%async_computation.7 | async-start | bytes 524288 | tf_op jit(solution)/shard_map/all_to_all | solution.py:125
  394.5 9.3 %all-to-all-done.7 = bf16[16,4,2048]{2,1,0:T(4,128)(2,1)S(1)} async-done(((bf16[16,4,2048]{2,1,0:T(4,128)(2,1)}), bf16[16,4,2048]{2,1,0:T(4,128)(2,1)S(1)}, u32[]{:S(2)}, u32[]{:S(2)}) %all-to-all-start.7) | async-done | bytes 262176 | tf_op jit(solution)/shard_map/all_to_all | solution.py:125
  (79 shorter events, 15.7 us)
Async XLA Ops:
  43.9 5.2 %copy-start.8 = (s32[16]{0:T(128)S(1)}, s32[16]{0:T(128)}, u32[]{:S(2)}) copy-start(s32[16]{0:T(128)} %param.16) | copy-start | bytes 196
  43.9 5.4 %copy-start.12 = (s32[2,16,1]{1,2,0:T(1,128)S(1)}, s32[2,16,1]{1,2,0:T(1,128)}, u32[]{:S(2)}) copy-start(s32[2,16,1]{1,2,0:T(1,128)} %param.14) | copy-start | bytes 388
  43.9 5.4 %copy-start.13 = (s32[2,16,1]{1,2,0:T(1,128)S(1)}, s32[2,16,1]{1,2,0:T(1,128)}, u32[]{:S(2)}) copy-start(s32[2,16,1]{1,2,0:T(1,128)} %param.13) | copy-start | bytes 388
  44.0 37.0 %all-to-all-start.5 = ((bf16[16,128,384]{2,1,0:T(8,128)(2,1)}), bf16[16,128,384]{2,1,0:T(8,128)(2,1)S(1)}, u32[]{:S(2)}, u32[]{:S(2)}) async-start(bf16[16,128,384]{2,1,0:T(8,128)(2,1)} %bitcast.91), calls=%async_computation.5 | async-start | bytes 3145728 | tf_op jit(solution)/shard_map/all_to_all | solution.py:93
  81.0 9.5 %copy-start.3 = (bf16[2,16,2048]{2,1,0:T(8,128)(2,1)S(1)}, bf16[2,16,2048]{2,1,0:T(8,128)(2,1)}, u32[]{:S(2)}) copy-start(bf16[2,16,2048]{2,1,0:T(8,128)(2,1)} %param.11) | copy-start | bytes 393220
  81.0 41.2 %all-to-all-start.1 = ((bf16[16,128,384]{2,1,0:T(8,128)(2,1)}), bf16[16,128,384]{2,1,0:T(8,128)(2,1)}, u32[]{:S(2)}, u32[]{:S(2)}) async-start(bf16[16,128,384]{2,1,0:T(8,128)(2,1)} %bitcast.92), calls=%async_computation.1 | async-start | bytes 3145728 | tf_op jit(solution)/shard_map/all_to_all | solution.py:83
  94.7 8.1 %copy-start.5 = (s32[1024]{0:T(1024)}, s32[1024]{0:T(1024)S(1)}, u32[]{:S(2)}) copy-start(s32[1024]{0:T(1024)S(1)} %pad_clamp_fusion.3) | copy-start | bytes 12292
  94.7 6.1 %copy-start.4 = (s32[1024]{0:T(1024)}, s32[1024]{0:T(1024)S(1)}, u32[]{:S(2)}) copy-start(s32[1024]{0:T(1024)S(1)} %pad_clamp_fusion.2) | copy-start | bytes 12292
  122.2 23.6 %all-to-all-start = ((bf16[16,4,2048]{2,1,0:T(4,128)(2,1)}), bf16[16,4,2048]{2,1,0:T(4,128)(2,1)S(1)}, u32[]{:S(2)}, u32[]{:S(2)}) async-start(bf16[16,4,2048]{2,1,0:T(4,128)(2,1)} %pad_maximum_fusion.3), calls=%async_computation | async-start | bytes 524288 | tf_op jit(solution)/shard_map/all_to_all | solution.py:79
  134.8 3.6 copy-start
  134.8 3.6 copy-start.1
  134.8 3.6 copy-start.6
  134.8 3.6 copy-start.7
  145.8 65.2 %all-to-all-start.2 = ((bf16[16,128,2,384]{3,1,2,0:T(8,128)(2,1)}), bf16[16,128,2,384]{3,1,2,0:T(8,128)(2,1)S(1)}, u32[]{:S(2)}, u32[]{:S(2)}) async-start(bf16[16,128,2,384]{3,1,2,0:T(8,128)(2,1)} %copy.26), calls=%async_computation.2 | async-start | bytes 6291456 | tf_op jit(solution)/shard_map/all_to_all | solution.py:114
  211.1 74.8 %all-to-all-start.4 = ((bf16[16,128,2,384]{3,1,2,0:T(8,128)(2,1)}), bf16[16,128,2,384]{3,1,2,0:T(8,128)(2,1)}, u32[]{:S(2)}, u32[]{:S(2)}) async-start(bf16[16,128,2,384]{3,1,2,0:T(8,128)(2,1)} %copy.28), calls=%async_computation.4 | async-start | bytes 6291456 | tf_op jit(solution)/shard_map/all_to_all | solution.py:115
  285.8 74.8 %all-to-all-start.6 = ((bf16[16,128,2,384]{3,1,2,0:T(8,128)(2,1)}), bf16[16,128,2,384]{3,1,2,0:T(8,128)(2,1)}, u32[]{:S(2)}, u32[]{:S(2)}) async-start(bf16[16,128,2,384]{3,1,2,0:T(8,128)(2,1)} %copy.30), calls=%async_computation.6 | async-start | bytes 6291456 | tf_op jit(solution)/shard_map/all_to_all | solution.py:116
  306.5 4.2 %copy-start.2 = (bf16[64,2048]{1,0:T(8,128)(2,1)S(1)}, bf16[64,2048]{1,0:T(8,128)(2,1)}, u32[]{:S(2)}) copy-start(bf16[64,2048]{1,0:T(8,128)(2,1)} %reshape.271) | copy-start | bytes 786436
  360.6 27.1 %all-to-all-start.8 = ((s32[16,1,4]{2,1,0:T(1,128)}), s32[16,1,4]{2,1,0:T(1,128)S(1)}, u32[]{:S(2)}, u32[]{:S(2)}) async-start(s32[16,1,4]{2,1,0:T(1,128)} %copy.34), calls=%async_computation.8 | async-start | bytes 16384 | tf_op jit(solution)/shard_map/all_to_all | solution.py:80
  381.2 12.6 %copy-start.10 = (s32[16]{0:T(128)S(1)}, s32[16]{0:T(128)}, u32[]{:S(2)}) copy-start(s32[16]{0:T(128)} %get-tuple-element.15) | copy-start | bytes 196
  381.2 12.6 %copy-start.9 = (s32[16]{0:T(128)S(1)}, s32[16]{0:T(128)}, u32[]{:S(2)}) copy-start(s32[16]{0:T(128)} %get-tuple-element.13) | copy-start | bytes 196
  381.2 12.6 %copy-start.11 = (f32[2,16,1]{1,2,0:T(1,128)S(1)}, f32[2,16,1]{1,2,0:T(1,128)}, u32[]{:S(2)}) copy-start(f32[2,16,1]{1,2,0:T(1,128)} %param.12) | copy-start | bytes 388
  387.8 16.0 %all-to-all-start.7 = ((bf16[16,4,2048]{2,1,0:T(4,128)(2,1)}), bf16[16,4,2048]{2,1,0:T(4,128)(2,1)S(1)}, u32[]{:S(2)}, u32[]{:S(2)}) async-start(bf16[16,4,2048]{2,1,0:T(4,128)(2,1)} %reshape.278), calls=%async_computation.7 | async-start | bytes 524288 | tf_op jit(solution)/shard_map/all_to_all | solution.py:125
where the time goes:
time: 407 us; the launch traced here: 406 us
  waiting for transfers between devices  212 us (52%)
  starting transfers between devices  82 us (20%)
  blocking collectives  43.3 us (11%)
  local copies, waits for them, and re-layouts  41.3 us (10%)
  other arithmetic  17.8 us (4%)
  matrix products  8.5 us (2%)
    all_to_all x1, waiting for transfers between devices, per_device(): lax.all_to_all(deliver(up_rows), 'expert', split_axis=0, concat_axis=0, t...  54.9 us
    all_to_all x1, waiting for transfers between devices, per_device(): lax.all_to_all(deliver(gate_rows), 'expert', split_axis=0, concat_axis=0,...  54.8 us
    all_to_all x1, waiting for transfers between devices, per_device(): lax.all_to_all(deliver(down_rows), 'expert', split_axis=0, concat_axis=0,...  46.3 us
    all_to_all x1, blocking collectives, per_device(): lax.all_to_all(up_panel.reshape(slots, block, half), 'expert', split_axis...  43.3 us
    all_to_all x1, waiting for transfers between devices, per_device(): lax.all_to_all(down_panel.reshape(slots, block, half), 'expert', split_ax...  29.4 us
    all_to_all x1, waiting for transfers between devices, per_device(): lax.all_to_all(gate_panel.reshape(slots, block, half), 'expert', split_ax...  17.5 us
    all_to_all x1, starting transfers between devices, per_device(): lax.all_to_all(deliver(down_rows), 'expert', split_axis=0, concat_axis=0,...  15.5 us
    all_to_all x1, starting transfers between devices, per_device(): lax.all_to_all(deliver(up_rows), 'expert', split_axis=0, concat_axis=0, t...  15.5 us
  transfers between devices with their start and end apart: 8, of which 6 were waited for; matrix products, arithmetic and copies ran while one was open for 16% of the time, Pallas kernels for 0%

commit v1 on v0

v1 whole, which is shorter than its diff:
```python
import jax
import jax.numpy as jnp
from jax import lax
from jax.sharding import PartitionSpec as P

LANES = 128


def slot_rank(new_expert, me):
    positions = jnp.arange(new_expert.shape[0], dtype=jnp.int32)
    mine = jnp.sum(jnp.where(positions == me, new_expert, 0))
    rank = jnp.sum(((new_expert == mine) & (positions < me)).astype(jnp.int32))
    return mine, rank


def per_device(
    activations,
    pick_weight,
    expert_ids,
    replica,
    old_home,
    new_expert,
    gate_panel,
    up_panel,
    down_panel,
):
    me = lax.axis_index("expert")
    batches, tokens, width = activations.shape
    top = expert_ids.shape[2]
    rows = batches * tokens
    x = activations.reshape(rows, width)
    picks = jnp.concatenate([expert_ids.reshape(rows, top), replica.reshape(rows, top)], axis=1)
    weights = pick_weight.reshape(rows, top)
    picks_all = lax.all_gather(picks, "expert", axis=0, tiled=True)
    weights_all = lax.all_gather(weights, "expert", axis=0, tiled=True)
    x_all = lax.all_gather(x, "expert", axis=0, tiled=True)
    ids_all = picks_all[:, :top]
    rep_all = picks_all[:, top:]
    mine, rank = slot_rank(new_expert, me)
    load = jnp.sum(((ids_all == mine) & (rep_all == rank)).astype(jnp.int32))
    labels = jnp.arange(old_home.shape[0], dtype=jnp.int32)
    held = jnp.sum(jnp.where(old_home == me // 2, labels, 0))
    scale = jnp.sum(jnp.where(ids_all == held, weights_all, 0.0), axis=1, keepdims=True)
    gate = jnp.dot(x_all, gate_panel[0], preferred_element_type=jnp.float32)
    up = jnp.dot(x_all, up_panel[0], preferred_element_type=jnp.float32)
    hidden = (jax.nn.silu(gate) * up).astype(jnp.bfloat16)
    part = lax.dot_general(
        hidden, down_panel[0], (((1,), (1,)), ((), ())), preferred_element_type=jnp.float32
    )
    part = (part * scale).astype(jnp.bfloat16)
    total = lax.psum_scatter(part, "expert", scatter_dimension=0, tiled=True)
    return total.reshape(batches, tokens, width), load.reshape(1)


def solution(mesh):
    return jax.shard_map(
        per_device,
        mesh=mesh,
        in_specs=(
            P(None, ("groups", "expert"), None),
            P(None, ("groups", "expert"), None),
            P(None, ("groups", "expert"), None),
            P(None, ("groups", "expert"), None),
            P(),
            P("groups"),
            P("expert", None, None),
            P("expert", None, None),
            P("expert", None, None),
        ),
        out_specs=(P(None, ("groups", "expert"), None), P(("groups", "expert"))),
        check_vma=False,
    )
```

time: 407 us -> 147 us (0.36)
  waiting for transfers between devices: 212 us -> 55.6 us
  starting transfers between devices: 82 us -> 0.08 us
  local copies, waits for them, and re-layouts: 41.3 us -> 3.49 us
  between operations: 0.94 us -> 14.7 us
  blocking collectives: 43.3 us -> 53 us
  other arithmetic: 17.8 us -> 9.75 us
    all_to_all x8 -> x0, waiting for transfers between devices: 212 us -> none  [the longest x1 54.9 us: per_device(): lax.all_to_all(deliver(up_rows), 'expert', split_axis=0, concat_axis=0, t...]
    all_to_all x8 -> x0, starting transfers between devices: 82 us -> none  [the longest x1 15.5 us: per_device(): lax.all_to_all(deliver(down_rows), 'expert', split_axis=0, concat_axis=0,...]
    reduce_scatter x0 -> x1, waiting for transfers between devices: none -> 54.9 us  [per_device(): total = lax.psum_scatter(part, 'expert', scatter_dimension=0, tiled=True)]
    all_to_all x1 -> x0, blocking collectives: 43.3 us -> none  [per_device(): lax.all_to_all(up_panel.reshape(slots, block, half), 'expert', split_axis...]
    unnamed x0 -> x1, blocking collectives: none -> 29.9 us
    all_gather x0 -> x1, blocking collectives: none -> 23.1 us  [per_device(): picks_all = lax.all_gather(picks, 'expert', axis=0, tiled=True)]
    gather x12 -> x0, local copies, waits for them, and re-layouts: 18.1 us -> none  [the longest x3 7.42 us: deliver(): jnp.take(pieces, second, axis=0)]
    all_to_all x4 -> x0, local copies, waits for them, and re-layouts: 13.5 us -> none  [the longest x1 5.1 us: per_device(): lax.all_to_all(deliver(down_rows), 'expert', split_axis=0, concat_axis=0,...]
  transfers between devices with their start and end apart: 8 -> 2, of which waited for: 6 -> 1; matrix products, arithmetic and copies ran while one was open for 16% -> 9% of each run, Pallas kernels for 0% -> 0%
where the time goes in v1:
time: 147 us; the launch traced here: 146 us
  waiting for transfers between devices  55.6 us (38%)
  blocking collectives  53 us (36%)
  between operations  14.7 us (10%)
  matrix products  9.76 us (7%)
  other arithmetic  9.75 us (7%)
  local copies, waits for them, and re-layouts  3.49 us (2%)
    reduce_scatter x1, waiting for transfers between devices, per_device(): total = lax.psum_scatter(part, 'expert', scatter_dimension=0, tiled=True)  54.9 us
    unnamed x1, blocking collectives  29.9 us
    all_gather x1, blocking collectives, per_device(): picks_all = lax.all_gather(picks, 'expert', axis=0, tiled=True)  23.1 us
    dot_general x1, matrix products, per_device(): lax.dot_general(hidden, down_panel[0], (((1,), (1,)), ((), ())), preferre...  5.48 us
    dot_general x1, matrix products, per_device(): gate = jnp.dot(x_all, gate_panel[0], preferred_element_type=jnp.float32)  4.28 us
    unnamed x4, other arithmetic  4.04 us
    unnamed x13, local copies, waits for them, and re-layouts  3.32 us
  transfers between devices with their start and end apart: 2, of which 1 were waited for; matrix products, arithmetic and copies ran while one was open for 9% of the time, Pallas kernels for 0%

profile of v1, /device:TPU:0, one launch (start us, length us, event | category | flops | bytes accessed | tf_op | source)
XLA Modules:
  0.0 146.4 jit_solution(16085344382893016342)
XLA Ops:
  7.2 0.0 copy-start
  7.2 0.0 all-gather.3.cloned.1.call-start
  7.2 0.7 all-gather.3.cloned.1.call-update
  7.9 0.0 reduce-scatter.2.cloned.1.call-start
  8.0 0.5 broadcast.13
  8.5 1.3 reduce.9
  9.8 0.1 reshape.30
  9.9 0.5 broadcast.14
  10.4 1.3 reduce.11
  11.8 0.1 reshape.25
  11.8 1.3 reduce.10
  13.2 0.1 reshape.26
  13.3 23.1 %all-gather = s32[16,32,2]{1,2,0:T(2,128)S(1)} all-gather(s32[1,32,2]{1,2,0:T(2,128)S(1)} %add_bitcast_fusion), channel_id=1, replica_groups=mesh['groups'=2,'expert'=16] {'expert'}, dimensions={0}, use_global_device_ids=true | all-gather | bytes 4352 | tf_op jit(solution)/shard_map/all_gather | solution.py:34
  36.4 0.1 reshape.34
  36.5 1.2 dynamic-slice
  38.4 0.2 dynamic-update-slice
  38.6 29.9 %all-reduce = f32[512]{0:T(512)S(1)} all-reduce(f32[512]{0:T(512)S(1)} %dynamic-update-slice), channel_id=1, replica_groups=mesh['groups'=2,'expert'=16] {'expert'}, use_global_device_ids=true, to_apply=%add | all-reduce | flops 512 | bytes 4096
  68.5 1.3 fusion.20
  69.8 0.6 compare_select_fusion
  70.5 0.0 copy-start.2
  70.5 0.0 all-gather.3.cloned.1.call-done
  70.5 4.3 %fusion.3 = f32[512,384]{1,0:T(8,128)} fusion(bf16[512,2048]{1,0:T(8,128)(2,1)} %all-gather.3.cloned.1.call-done, bf16[1,2048,384]{2,1,0:T(8,128)(2,1)} %param.15), kind=kOutput, calls=%fused_computation.4 | convolution fusion | flops 805306368 | bytes 4456448 | tf_op jit(solution)/shard_map/dot_general | solution.py:44
  74.8 0.0 copy-done
  74.8 0.0 copy-done.2
  74.8 5.5 %multiply_convert_fusion = bf16[512,2048]{1,0:T(8,128)(2,1)} fusion(f32[512]{0:T(512)S(1)} %bitcast.32, bf16[1,2048,384]{2,1,0:T(8,128)(2,1)S(1)} %copy-done, bf16[512,2048]{1,0:T(8,128)(2,1)} %all-gather.3.cloned.1.call-done, bf16[1,2048,384]{2,1,0:T(8,128)(2,1)S(1)} %copy-done.2, f32[512,384]{1,0:T(8,128)} %fusion.3), kind=kOutput, calls=%fused_computation | convolution fusion | flops 1613889536 | bytes 8128512 | tf_op jit(solution)/shard_map/dot_general | solution.py:47
  80.3 0.0 copy-start.1
  80.3 0.0 reduce-scatter.2.cloned.1.call-update
  80.3 0.6 copy-done.1
  81.0 0.6 fusion.21
  81.6 1.3 fusion.22
  82.9 1.9 %fusion.19 = s32[]{:T(128)} fusion(s32[512,2]{0,1:T(2,128)S(1)} %reshape.34, s32[]{:T(128)} %fusion.22, s32[]{:T(128)} %fusion.21), kind=kLoop, calls=%fused_computation.19 | loop fusion | flops 2559 | bytes 4108 | tf_op jit(solution)/shard_map/reduce_sum | solution.py:40
  84.7 54.9 %reduce-scatter.2.cloned.1.call-done = bf16[32,2048]{1,0:T(8,128)(2,1)} async-done(((bf16[512,2048]{1,0:T(8,128)(2,1)}), bf16[32,2048]{1,0:T(8,128)(2,1)}) %reduce-scatter.2.cloned.1.call-update) | async-done | bytes 131088 | tf_op jit(solution)/shard_map/reduce_scatter | solution.py:51
  (3 shorter events, 0.0 us)
Async XLA Ops:
  7.2 67.7 %copy-start = (bf16[1,2048,384]{2,1,0:T(8,128)(2,1)S(1)}, bf16[1,2048,384]{2,1,0:T(8,128)(2,1)}, u32[]{:S(2)}) copy-start(bf16[1,2048,384]{2,1,0:T(8,128)(2,1)} %param.17) | copy-start | bytes 4718596
  7.2 63.3 %all-gather.3.cloned.1.call-start = ((), (), s32[]{:S(2)}) async-start(), calls=%async_computation.1 | async-start | bytes 2228224 | tf_op jit(solution)/shard_map/all_gather | solution.py:36
  7.9 131.7 %reduce-scatter.2.cloned.1.call-start = ((), (), s32[]{:S(2)}) async-start(), calls=%async_computation.2 | async-start | bytes 2228224 | tf_op jit(solution)/shard_map/reduce_scatter | solution.py:51
  70.5 4.3 %copy-start.2 = (bf16[1,2048,384]{2,1,0:T(8,128)(2,1)S(1)}, bf16[1,2048,384]{2,1,0:T(8,128)(2,1)}, u32[]{:S(2)}) copy-start(bf16[1,2048,384]{2,1,0:T(8,128)(2,1)} %param.16) | copy-start | bytes 4718596
  80.3 0.7 copy-start.1
Sparse Core Ops, SparseCore 0:
  10.1 44.4 all-gather.2
  80.4 59.1 reduce-scatter.1
